TPU v7x, 32 devices: a whole 2x2x4 slice. The times are simulated.
32 devices in a mesh: il: 16 (over z, y, core), xl: 2 (over x).
Axes of the slice: x: 2, y: 2, z: 4, core: 2. Of those that a mesh axis runs over, the one named last changes fastest.
Arguments:
- solution: float32 [64, 128, 512], P('il', 'xl'), may hold values from -6 to 6
- residual: float32 [64, 128, 512], P('il', 'xl'), may hold values from -30 to 30
- direction: float32 [64, 128, 512], P('il', 'xl'), may hold values from -30 to 30
- slope_il: float32 [64, 128, 512], P('il', 'xl'), may hold values from -1.5 to 1.5
- slope_xl: float32 [64, 128, 512], P('il', 'xl'), may hold values from -1.5 to 1.5
- weights: float32 [64, 128, 512], P('il', 'xl'), may hold values from 0.2 to 1
Outputs:
- new_solution: float32 [64, 128, 512], P('il', 'xl')
- new_residual: float32 [64, 128, 512], P('il', 'xl')
- new_direction: float32 [64, 128, 512], P('il', 'xl')
All inputs are finite; a program needn't handle non-finite values.
Results may differ from a plain program's by a relative error of at most 0.00002.
Values sent between devices are 32-bit elements; how exact they have to be, the bound alone decides.
No kernel may reach another device: no remote copies, remote signals or barrier semaphores. Data moves between devices by JAX's collectives and lax.ppermute only.
A program may use at most 64 MiB of HBM per device.

v0:
```python
import jax
import jax.numpy as jnp
from jax import lax
from jax.sharding import PartitionSpec as P

damping = 0.3


def padded_2(value, sides, width):
    for axis, dim in sides:
        size, length = (lax.axis_size(axis), value.shape[dim])
        up = [(i, (i + 1) % size) for i in range(size - 1)]
        down = [(j, i) for i, j in up]
        last = lax.slice_in_dim(value, length - width, length, axis=dim)
        first = lax.slice_in_dim(value, 0, width, axis=dim)
        before = lax.ppermute(last, axis, up)
        after = lax.ppermute(first, axis, down)
        value = jnp.concatenate([before, value, after], axis=dim)
    return value


def shifted(value, axis, by):
    length = lax.axis_size(axis)
    pairs = [(i, i + by) for i in range(length) if 0 <= i + by < length]
    return lax.ppermute(value, axis, pairs)


def time_diff(field):
    padded = jnp.pad(field, ((0, 0), (0, 0), (1, 1)))
    return 0.5 * (padded[:, :, 2:] - padded[:, :, :-2])


def normal_apply(direction, slope_il, slope_xl, weights):
    il_rows = direction.shape[0]
    xl_rows = direction.shape[1]
    total_il = il_rows * lax.axis_size("il")
    total_xl = xl_rows * lax.axis_size("xl")
    start_il = lax.axis_index("il") * il_rows
    start_xl = lax.axis_index("xl") * xl_rows
    field = padded_2(direction, (("il", 0), ("xl", 1)), 1)
    coef_il = shifted(jnp.stack([slope_il[-1:], weights[-1:]]), "il", 1)
    coef_xl = shifted(jnp.stack([slope_xl[:, -1:], weights[:, -1:]]), "xl", 1)
    current = field[:-1, 1:-1]
    slope_rows = jnp.concatenate([coef_il[0], slope_il], 0)
    weight_rows = jnp.concatenate([coef_il[1], weights], 0)
    global_il = start_il - 1 + jnp.arange(il_rows + 1)
    keep_il = (global_il < total_il - 1)[:, None, None]
    flux_il = jnp.where(
        keep_il,
        weight_rows * weight_rows * (field[1:, 1:-1] - current - slope_rows * time_diff(current)),
        0.0,
    )
    current = field[1:-1, :-1]
    slope_cols = jnp.concatenate([coef_xl[0], slope_xl], 1)
    weight_cols = jnp.concatenate([coef_xl[1], weights], 1)
    global_xl = start_xl - 1 + jnp.arange(xl_rows + 1)
    keep_xl = (global_xl < total_xl - 1)[None, :, None]
    flux_xl = jnp.where(
        keep_xl,
        weight_cols * weight_cols * (field[1:-1, 1:] - current - slope_cols * time_diff(current)),
        0.0,
    )
    term_il = flux_il[:-1] - flux_il[1:] + time_diff(slope_il * flux_il[1:])
    term_xl = flux_xl[:, :-1] - flux_xl[:, 1:] + time_diff(slope_xl * flux_xl[:, 1:])
    return term_il + term_xl + damping * direction


def body(solution, residual, direction, slope_il, slope_xl, weights):
    image = normal_apply(direction, slope_il, slope_xl, weights)
    norm_old, along, cross_term, image_norm = lax.psum(
        (
            jnp.sum(residual * residual),
            jnp.sum(direction * image),
            jnp.sum(residual * image),
            jnp.sum(image * image),
        ),
        ("il", "xl"),
    )
    alpha = norm_old / along
    new_residual = residual - alpha * image
    norm_new = norm_old - 2.0 * alpha * cross_term + alpha * alpha * image_norm
    new_solution = solution + alpha * direction
    new_direction = new_residual + norm_new / norm_old * direction
    return (new_solution, new_residual, new_direction)


def solution(mesh):
    placed = (
        P("il", "xl", None),
        P("il", "xl", None),
        P("il", "xl", None),
        P("il", "xl", None),
        P("il", "xl", None),
        P("il", "xl", None),
    )
    return jax.shard_map(
        body,
        mesh=mesh,
        in_specs=placed,
        out_specs=(P("il", "xl", None), P("il", "xl", None), P("il", "xl", None)),
        check_vma=False,
    )
```

profile of v0, /device:TPU:0, one launch (start us, length us, event | category | flops | bytes accessed | tf_op | source)
XLA Modules:
  0.0 73.8 jit_solution(13311208214205433469)
XLA Ops:
  0.6 0.0 copy-start.1
  0.6 1.0 %fusion.23 = (f32[1,64,512]{2,1,0:T(8,128)S(1)}, f32[1,64,512]{2,1,0:T(8,128)S(1)}) fusion(f32[4,64,512]{2,1,0:T(8,128)} %param.8), kind=kLoop, calls=%fused_computation.63 | loop fusion | bytes 524288 | tf_op jit(solution)/shard_map/slice | solution.py:15
  1.7 2.4 %collective-permute-start.2 = (f32[1,64,512]{2,1,0:T(8,128)S(1)}, f32[1,64,512]{2,1,0:T(8,128)S(1)}, u32[]{:S(2)}, u32[]{:S(2)}) collective-permute-start(f32[1,64,512]{2,1,0:T(8,128)S(1)} %get-tuple-element.20), channel_id=1, source_target_pairs={{0,2},{2,4},{4,6},{6,8},{8,10},{10,12},{12,14},{14,16},{16,18},{18... | collective-permute-start | bytes 393224 | tf_op jit(solution)/shard_map/ppermute | solution.py:16
  4.1 1.3 %collective-permute-start.1 = (f32[1,64,512]{2,1,0:T(8,128)S(1)}, f32[1,64,512]{2,1,0:T(8,128)S(1)}, u32[]{:S(2)}, u32[]{:S(2)}) collective-permute-start(f32[1,64,512]{2,1,0:T(8,128)S(1)} %get-tuple-element.19), channel_id=1, source_target_pairs={{2,0},{4,2},{6,4},{8,6},{10,8},{12,10},{14,12},{16,14},{18,16},{20... | collective-permute-start | bytes 393224 | tf_op jit(solution)/shard_map/ppermute | solution.py:17
  5.4 0.0 copy-done.1
  5.4 0.9 %slice_bitcast_fusion.7 = f32[1,4,1,512]{3,2,1,0:T(1,128)S(1)} fusion(f32[4,64,512]{2,1,0:T(8,128)} %param.10), kind=kLoop, calls=%fused_computation.59 | loop fusion | bytes 16384 | tf_op jit(solution)/shard_map/stack | solution.py:42
  6.3 4.2 %collective-permute-start.3 = (f32[2,4,1,512]{3,2,1,0:T(1,128)S(1)}, f32[2,4,1,512]{3,2,1,0:T(1,128)S(1)}, u32[]{:S(2)}, u32[]{:S(2)}) collective-permute-start(f32[2,4,1,512]{3,2,1,0:T(1,128)S(1)} %pad_maximum_fusion.3), channel_id=1, source_target_pairs={{0,1},{2,3},{4,5},{6,7},{8,9},{10,11},{12,13},{14,15},{16,17},{18,... | collective-permute-start | bytes 49160 | tf_op jit(solution)/shard_map/ppermute | solution.py:25
  10.5 0.9 %slice_bitcast_fusion.3 = f32[1,1,64,512]{3,2,1,0:T(8,128)S(1)} fusion(f32[4,64,512]{2,1,0:T(8,128)} %param.9), kind=kLoop, calls=%fused_computation.49 | loop fusion | bytes 262144 | tf_op jit(solution)/shard_map/stack | solution.py:41
  11.5 0.0 copy-start
  11.5 4.2 %collective-permute-start = (f32[2,1,64,512]{3,2,1,0:T(8,128)S(1)}, f32[2,1,64,512]{3,2,1,0:T(8,128)S(1)}, u32[]{:S(2)}, u32[]{:S(2)}) collective-permute-start(f32[2,1,64,512]{3,2,1,0:T(8,128)S(1)} %pad_maximum_fusion.2), channel_id=1, source_target_pairs={{0,2},{2,4},{4,6},{6,8},{8,10},{10,12},{12,14},{14,16},{16,18},{18... | collective-permute-start | bytes 786440 | tf_op jit(solution)/shard_map/ppermute | solution.py:25
  15.7 0.0 collective-permute-done.2
  15.8 0.0 copy-done
  15.8 0.1 constant_dynamic-update-slice_fusion
  15.9 0.0 collective-permute-done.1
  15.9 1.6 %collective-permute-start.5 = (f32[6,1,512]{2,1,0:T(1,128)S(1)}, f32[6,1,512]{2,1,0:T(1,128)S(1)}, u32[]{:S(2)}, u32[]{:S(2)}) collective-permute-start(f32[6,1,512]{2,1,0:T(1,128)S(1)} %get-tuple-element.15), channel_id=1, source_target_pairs={{0,1},{2,3},{4,5},{6,7},{8,9},{10,11},{12,13},{14,15},{16,17},{18,... | collective-permute-start | bytes 36872 | tf_op jit(solution)/shard_map/ppermute | solution.py:16
  17.5 0.0 collective-permute-done.3
  17.5 0.0 copy-start.3
  17.5 1.4 %collective-permute-start.4 = (f32[6,1,512]{2,1,0:T(1,128)S(1)}, f32[6,1,512]{2,1,0:T(1,128)S(1)}, u32[]{:S(2)}, u32[]{:S(2)}) collective-permute-start(f32[6,1,512]{2,1,0:T(1,128)S(1)} %get-tuple-element.14), channel_id=1, source_target_pairs={{1,0},{3,2},{5,4},{7,6},{9,8},{11,10},{13,12},{15,14},{17,16},{19,... | collective-permute-start | bytes 36872 | tf_op jit(solution)/shard_map/ppermute | solution.py:17
  19.0 0.0 collective-permute-done.5
  19.0 0.1 pad_maximum_fusion
  19.1 4.2 %collective-permute-done.4 = f32[6,1,512]{2,1,0:T(1,128)S(1)} collective-permute-done((f32[6,1,512]{2,1,0:T(1,128)S(1)}, f32[6,1,512]{2,1,0:T(1,128)S(1)}, u32[]{:S(2)}, u32[]{:S(2)}) %collective-permute-start.4) | collective-permute-done | bytes 12320 | tf_op jit(solution)/shard_map/ppermute | solution.py:17
  23.3 0.0 copy-done.3
  23.3 0.5 fusion.11
  23.8 0.1 slice_multiply_fusion
  23.9 0.0 copy-start.2
  23.9 0.0 collective-permute-done
  23.9 1.0 %copy-done.2 = f32[4,64,512]{2,1,0:T(8,128)S(1)} copy-done((f32[4,64,512]{2,1,0:T(8,128)S(1)}, f32[4,64,512]{2,1,0:T(8,128)}, u32[]{:S(2)}) %copy-start.2) | copy-done | bytes 524312
  24.9 0.5 fusion.5
  25.4 0.0 copy-start.4
  25.4 0.1 slice_multiply_fusion.1
  25.5 0.9 %copy-done.4 = f32[4,64,512]{2,1,0:T(8,128)S(1)} copy-done((f32[4,64,512]{2,1,0:T(8,128)S(1)}, f32[4,64,512]{2,1,0:T(8,128)}, u32[]{:S(2)}) %copy-start.4) | copy-done | bytes 524312
  26.5 0.0 copy-start.5
  26.5 1.3 %multiply_reduce_fusion = (f32[]{:T(128)}, f32[]{:T(128)}, f32[]{:T(128)}, f32[]{:T(128)}, f32[4,64,512]{2,1,0:T(8,128)S(1)}) fusion(f32[4,64,512]{2,1,0:T(8,128)S(1)} %copy-done.4, f32[4,64,512]{2,1,0:T(8,128)S(1)} %copy-done, f32[4,64,512]{2,1,0:T(8,128)S(1)} %slice_multiply_fusion, f32[4,65,512]{2,1,0:T(8,128)S(1)} %fusion.11, ...), kind=kLoop, calls=%fused_computation.37 | loop fusion | flops 2490364 | bytes 4718608 | tf_op jit(solution)/shard_map/reduce_sum | solution.py:75
  27.8 40.8 %all-reduce.4 = (f32[]{:T(128)}, f32[]{:T(128)}, f32[]{:T(128)}, f32[]{:T(128)}) all-reduce(f32[]{:T(128)} %get-tuple-element.5, f32[]{:T(128)} %get-tuple-element.6, f32[]{:T(128)} %get-tuple-element.4, f32[]{:T(128)} %get-tuple-element.3), channel_id=1, replica_groups=mesh['il'=16,'xl'=2] {'il','xl'}, use_global_device_ids=true, to_apply=%region_1.2 | all-reduce | flops 4 | bytes 32 | tf_op jit(solution)/shard_map/psum | solution.py:70
  72.5 0.0 copy-done.5
  72.5 1.4 %multiply_add_fusion = (f32[4,64,512]{2,1,0:T(8,128)}, f32[4,64,512]{2,1,0:T(8,128)}, f32[4,64,512]{2,1,0:T(8,128)}) fusion(f32[4,64,512]{2,1,0:T(8,128)S(1)} %copy-done, f32[]{:T(128)S(6)} %div.7, f32[4,64,512]{2,1,0:T(8,128)S(1)} %copy-done.4, f32[4,64,512]{2,1,0:T(8,128)S(1)} %get-tuple-element.13, f32[]{:T(128)S(6)} %div.6, f32[4,64,512]{2,1,0:T(8,128)S(1)} %copy-done.5), kind=kLoop, calls=%fused_computation.36 | loop fusion | flops 786432 | bytes 3670024 | tf_op jit(solution)/shard_map/add | solution.py:83
  (11 shorter events, 0.1 us)
Async XLA Ops:
  0.6 4.8 %copy-start.1 = (f32[4,64,512]{2,1,0:T(8,128)S(1)}, f32[4,64,512]{2,1,0:T(8,128)}, u32[]{:S(2)}) copy-start(f32[4,64,512]{2,1,0:T(8,128)} %param.11) | copy-start | bytes 1572868
  1.7 14.1 %collective-permute-start.2 = (f32[1,64,512]{2,1,0:T(8,128)S(1)}, f32[1,64,512]{2,1,0:T(8,128)S(1)}, u32[]{:S(2)}, u32[]{:S(2)}) collective-permute-start(f32[1,64,512]{2,1,0:T(8,128)S(1)} %get-tuple-element.20), channel_id=1, source_target_pairs={{0,2},{2,4},{4,6},{6,8},{8,10},{10,12},{12,14},{14,16},{16,18},{18... | collective-permute-start | bytes 393224 | tf_op jit(solution)/shard_map/ppermute | solution.py:16
  4.1 11.8 %collective-permute-start.1 = (f32[1,64,512]{2,1,0:T(8,128)S(1)}, f32[1,64,512]{2,1,0:T(8,128)S(1)}, u32[]{:S(2)}, u32[]{:S(2)}) collective-permute-start(f32[1,64,512]{2,1,0:T(8,128)S(1)} %get-tuple-element.19), channel_id=1, source_target_pairs={{2,0},{4,2},{6,4},{8,6},{10,8},{12,10},{14,12},{16,14},{18,16},{20... | collective-permute-start | bytes 393224 | tf_op jit(solution)/shard_map/ppermute | solution.py:17
  6.3 11.2 %collective-permute-start.3 = (f32[2,4,1,512]{3,2,1,0:T(1,128)S(1)}, f32[2,4,1,512]{3,2,1,0:T(1,128)S(1)}, u32[]{:S(2)}, u32[]{:S(2)}) collective-permute-start(f32[2,4,1,512]{3,2,1,0:T(1,128)S(1)} %pad_maximum_fusion.3), channel_id=1, source_target_pairs={{0,1},{2,3},{4,5},{6,7},{8,9},{10,11},{12,13},{14,15},{16,17},{18,... | collective-permute-start | bytes 49160 | tf_op jit(solution)/shard_map/ppermute | solution.py:25
  11.5 4.3 %copy-start = (f32[4,64,512]{2,1,0:T(8,128)S(1)}, f32[4,64,512]{2,1,0:T(8,128)}, u32[]{:S(2)}) copy-start(f32[4,64,512]{2,1,0:T(8,128)} %param.8) | copy-start | bytes 1572868
  11.5 12.4 %collective-permute-start = (f32[2,1,64,512]{3,2,1,0:T(8,128)S(1)}, f32[2,1,64,512]{3,2,1,0:T(8,128)S(1)}, u32[]{:S(2)}, u32[]{:S(2)}) collective-permute-start(f32[2,1,64,512]{3,2,1,0:T(8,128)S(1)} %pad_maximum_fusion.2), channel_id=1, source_target_pairs={{0,2},{2,4},{4,6},{6,8},{8,10},{10,12},{12,14},{14,16},{16,18},{18... | collective-permute-start | bytes 786440 | tf_op jit(solution)/shard_map/ppermute | solution.py:25
  15.9 3.0 %collective-permute-start.5 = (f32[6,1,512]{2,1,0:T(1,128)S(1)}, f32[6,1,512]{2,1,0:T(1,128)S(1)}, u32[]{:S(2)}, u32[]{:S(2)}) collective-permute-start(f32[6,1,512]{2,1,0:T(1,128)S(1)} %get-tuple-element.15), channel_id=1, source_target_pairs={{0,1},{2,3},{4,5},{6,7},{8,9},{10,11},{12,13},{14,15},{16,17},{18,... | collective-permute-start | bytes 36872 | tf_op jit(solution)/shard_map/ppermute | solution.py:16
  17.5 5.7 %copy-start.3 = (f32[4,64,512]{2,1,0:T(8,128)S(1)}, f32[4,64,512]{2,1,0:T(8,128)}, u32[]{:S(2)}) copy-start(f32[4,64,512]{2,1,0:T(8,128)} %param.10) | copy-start | bytes 1572868
  17.5 5.7 %collective-permute-start.4 = (f32[6,1,512]{2,1,0:T(1,128)S(1)}, f32[6,1,512]{2,1,0:T(1,128)S(1)}, u32[]{:S(2)}, u32[]{:S(2)}) collective-permute-start(f32[6,1,512]{2,1,0:T(1,128)S(1)} %get-tuple-element.14), channel_id=1, source_target_pairs={{1,0},{3,2},{5,4},{7,6},{9,8},{11,10},{13,12},{15,14},{17,16},{19,... | collective-permute-start | bytes 36872 | tf_op jit(solution)/shard_map/ppermute | solution.py:17
  23.9 1.0 %copy-start.2 = (f32[4,64,512]{2,1,0:T(8,128)S(1)}, f32[4,64,512]{2,1,0:T(8,128)}, u32[]{:S(2)}) copy-start(f32[4,64,512]{2,1,0:T(8,128)} %param.9) | copy-start | bytes 1572868
  25.4 1.0 %copy-start.4 = (f32[4,64,512]{2,1,0:T(8,128)S(1)}, f32[4,64,512]{2,1,0:T(8,128)}, u32[]{:S(2)}) copy-start(f32[4,64,512]{2,1,0:T(8,128)} %param.7) | copy-start | bytes 1572868
  26.5 46.0 %copy-start.5 = (f32[4,64,512]{2,1,0:T(8,128)S(1)}, f32[4,64,512]{2,1,0:T(8,128)}, u32[]{:S(2)}) copy-start(f32[4,64,512]{2,1,0:T(8,128)} %param.6) | copy-start | bytes 1572868
where the time goes:
time: 74.4 us; the launch traced here: 73.8 us
  blocking collectives  40.8 us (55%)
  starting transfers between devices  15.1 us (20%)
  local copies, waits for them, and re-layouts  4.96 us (7%)
  between operations  4.8 us (6%)
  waiting for transfers between devices  4.21 us (6%)
  other arithmetic  3.96 us (5%)
    psum x1, blocking collectives, body(): lax.psum((jnp.sum(residual * residual), jnp.sum(direction * image), jnp.s...  40.8 us
    ppermute x2, starting transfers between devices, shifted(): return lax.ppermute(value, axis, pairs)  8.41 us
    ppermute x2, waiting for transfers between devices, padded_2(): after = lax.ppermute(first, axis, down)  4.2 us
    ppermute x2, starting transfers between devices, padded_2(): before = lax.ppermute(last, axis, up)  3.98 us
    ppermute x2, starting transfers between devices, padded_2(): after = lax.ppermute(first, axis, down)  2.72 us
    unnamed x13, local copies, waits for them, and re-layouts  1.99 us
  transfers between devices with their start and end apart: 6, of which 1 were waited for; matrix products, arithmetic and copies ran while one was open for 4% of the time, Pallas kernels for 0%

commit v1 on v0

--- a/solution.py
+++ b/solution.py
@@ -4,6 +4,11 @@
 from jax.sharding import PartitionSpec as P
 
 damping = 0.3
+
+
+def by_each_axis(x, leading, second):
+    partial = lax.psum(x, leading)
+    return lax.psum(partial, second)
 
 
 def padded_2(value, sides, width):
@@ -67,14 +72,15 @@
 
 def body(solution, residual, direction, slope_il, slope_xl, weights):
     image = normal_apply(direction, slope_il, slope_xl, weights)
-    norm_old, along, cross_term, image_norm = lax.psum(
+    norm_old, along, cross_term, image_norm = by_each_axis(
         (
             jnp.sum(residual * residual),
             jnp.sum(direction * image),
             jnp.sum(residual * image),
             jnp.sum(image * image),
         ),
-        ("il", "xl"),
+        "xl",
+        "il",
     )
     alpha = norm_old / along
     new_residual = residual - alpha * image

time: 74.4 us -> 69.2 us (0.930)
  blocking collectives: 40.8 us -> 35.8 us
    psum x1 -> x2, blocking collectives: 40.8 us -> 35.8 us  [the longest x1 30.2 us: by_each_axis(): return lax.psum(partial, second)]
where the time goes in v1:
time: 69.2 us; the launch traced here: 68.7 us
  blocking collectives  35.8 us (52%)
  starting transfers between devices  15.1 us (22%)
  local copies, waits for them, and re-layouts  4.96 us (7%)
  between operations  4.79 us (7%)
  waiting for transfers between devices  4.21 us (6%)
  other arithmetic  3.88 us (6%)
    psum x1, blocking collectives, by_each_axis(): return lax.psum(partial, second)  30.2 us
    ppermute x2, starting transfers between devices, shifted(): return lax.ppermute(value, axis, pairs)  8.41 us
    psum x1, blocking collectives, by_each_axis(): partial = lax.psum(x, leading)  5.56 us
    ppermute x2, waiting for transfers between devices, padded_2(): after = lax.ppermute(first, axis, down)  4.2 us
    ppermute x2, starting transfers between devices, padded_2(): before = lax.ppermute(last, axis, up)  3.98 us
    ppermute x2, starting transfers between devices, padded_2(): after = lax.ppermute(first, axis, down)  2.72 us
    unnamed x13, local copies, waits for them, and re-layouts  1.99 us
  transfers between devices with their start and end apart: 6, of which 1 were waited for; matrix products, arithmetic and copies ran while one was open for 4% of the time, Pallas kernels for 0%

profile of v1, /device:TPU:0, one launch (start us, length us, event | category | flops | bytes accessed | tf_op | source)
XLA Modules:
  0.0 68.7 jit_solution(1682389726481165762)
XLA Ops:
  0.6 0.0 copy-start.1
  0.6 1.0 %fusion.23 = (f32[1,64,512]{2,1,0:T(8,128)S(1)}, f32[1,64,512]{2,1,0:T(8,128)S(1)}) fusion(f32[4,64,512]{2,1,0:T(8,128)} %param.8), kind=kLoop, calls=%fused_computation.63 | loop fusion | bytes 524288 | tf_op jit(solution)/shard_map/slice | solution.py:20
  1.7 2.4 %collective-permute-start.2 = (f32[1,64,512]{2,1,0:T(8,128)S(1)}, f32[1,64,512]{2,1,0:T(8,128)S(1)}, u32[]{:S(2)}, u32[]{:S(2)}) collective-permute-start(f32[1,64,512]{2,1,0:T(8,128)S(1)} %get-tuple-element.24), channel_id=1, source_target_pairs={{0,2},{2,4},{4,6},{6,8},{8,10},{10,12},{12,14},{14,16},{16,18},{18... | collective-permute-start | bytes 393224 | tf_op jit(solution)/shard_map/ppermute | solution.py:21
  4.1 1.3 %collective-permute-start.1 = (f32[1,64,512]{2,1,0:T(8,128)S(1)}, f32[1,64,512]{2,1,0:T(8,128)S(1)}, u32[]{:S(2)}, u32[]{:S(2)}) collective-permute-start(f32[1,64,512]{2,1,0:T(8,128)S(1)} %get-tuple-element.23), channel_id=1, source_target_pairs={{2,0},{4,2},{6,4},{8,6},{10,8},{12,10},{14,12},{16,14},{18,16},{20... | collective-permute-start | bytes 393224 | tf_op jit(solution)/shard_map/ppermute | solution.py:22
  5.4 0.0 copy-done.1
  5.4 0.9 %slice_bitcast_fusion.7 = f32[1,4,1,512]{3,2,1,0:T(1,128)S(1)} fusion(f32[4,64,512]{2,1,0:T(8,128)} %param.10), kind=kLoop, calls=%fused_computation.59 | loop fusion | bytes 16384 | tf_op jit(solution)/shard_map/stack | solution.py:47
  6.3 4.2 %collective-permute-start.3 = (f32[2,4,1,512]{3,2,1,0:T(1,128)S(1)}, f32[2,4,1,512]{3,2,1,0:T(1,128)S(1)}, u32[]{:S(2)}, u32[]{:S(2)}) collective-permute-start(f32[2,4,1,512]{3,2,1,0:T(1,128)S(1)} %pad_maximum_fusion.3), channel_id=1, source_target_pairs={{0,1},{2,3},{4,5},{6,7},{8,9},{10,11},{12,13},{14,15},{16,17},{18,... | collective-permute-start | bytes 49160 | tf_op jit(solution)/shard_map/ppermute | solution.py:30
  10.5 0.9 %slice_bitcast_fusion.3 = f32[1,1,64,512]{3,2,1,0:T(8,128)S(1)} fusion(f32[4,64,512]{2,1,0:T(8,128)} %param.9), kind=kLoop, calls=%fused_computation.49 | loop fusion | bytes 262144 | tf_op jit(solution)/shard_map/stack | solution.py:46
  11.5 0.0 copy-start
  11.5 4.2 %collective-permute-start = (f32[2,1,64,512]{3,2,1,0:T(8,128)S(1)}, f32[2,1,64,512]{3,2,1,0:T(8,128)S(1)}, u32[]{:S(2)}, u32[]{:S(2)}) collective-permute-start(f32[2,1,64,512]{3,2,1,0:T(8,128)S(1)} %pad_maximum_fusion.2), channel_id=1, source_target_pairs={{0,2},{2,4},{4,6},{6,8},{8,10},{10,12},{12,14},{14,16},{16,18},{18... | collective-permute-start | bytes 786440 | tf_op jit(solution)/shard_map/ppermute | solution.py:30
  15.7 0.0 collective-permute-done.2
  15.8 0.0 copy-done
  15.8 0.1 constant_dynamic-update-slice_fusion
  15.9 0.0 collective-permute-done.1
  15.9 1.6 %collective-permute-start.5 = (f32[6,1,512]{2,1,0:T(1,128)S(1)}, f32[6,1,512]{2,1,0:T(1,128)S(1)}, u32[]{:S(2)}, u32[]{:S(2)}) collective-permute-start(f32[6,1,512]{2,1,0:T(1,128)S(1)} %get-tuple-element.19), channel_id=1, source_target_pairs={{0,1},{2,3},{4,5},{6,7},{8,9},{10,11},{12,13},{14,15},{16,17},{18,... | collective-permute-start | bytes 36872 | tf_op jit(solution)/shard_map/ppermute | solution.py:21
  17.5 0.0 collective-permute-done.3
  17.5 0.0 copy-start.3
  17.5 1.4 %collective-permute-start.4 = (f32[6,1,512]{2,1,0:T(1,128)S(1)}, f32[6,1,512]{2,1,0:T(1,128)S(1)}, u32[]{:S(2)}, u32[]{:S(2)}) collective-permute-start(f32[6,1,512]{2,1,0:T(1,128)S(1)} %get-tuple-element.18), channel_id=1, source_target_pairs={{1,0},{3,2},{5,4},{7,6},{9,8},{11,10},{13,12},{15,14},{17,16},{19,... | collective-permute-start | bytes 36872 | tf_op jit(solution)/shard_map/ppermute | solution.py:22
  19.0 0.0 collective-permute-done.5
  19.0 0.1 pad_maximum_fusion
  19.1 4.2 %collective-permute-done.4 = f32[6,1,512]{2,1,0:T(1,128)S(1)} collective-permute-done((f32[6,1,512]{2,1,0:T(1,128)S(1)}, f32[6,1,512]{2,1,0:T(1,128)S(1)}, u32[]{:S(2)}, u32[]{:S(2)}) %collective-permute-start.4) | collective-permute-done | bytes 12320 | tf_op jit(solution)/shard_map/ppermute | solution.py:22
  23.3 0.0 copy-done.3
  23.3 0.5 fusion.11
  23.8 0.1 slice_multiply_fusion
  23.9 0.0 copy-start.2
  23.9 0.0 collective-permute-done
  23.9 1.0 %copy-done.2 = f32[4,64,512]{2,1,0:T(8,128)S(1)} copy-done((f32[4,64,512]{2,1,0:T(8,128)S(1)}, f32[4,64,512]{2,1,0:T(8,128)}, u32[]{:S(2)}) %copy-start.2) | copy-done | bytes 524312
  24.9 0.5 fusion.5
  25.4 0.0 copy-start.4
  25.4 0.1 slice_multiply_fusion.1
  25.5 0.9 %copy-done.4 = f32[4,64,512]{2,1,0:T(8,128)S(1)} copy-done((f32[4,64,512]{2,1,0:T(8,128)S(1)}, f32[4,64,512]{2,1,0:T(8,128)}, u32[]{:S(2)}) %copy-start.4) | copy-done | bytes 524312
  26.5 0.0 copy-start.5
  26.5 1.2 %multiply_reduce_fusion = (f32[]{:T(128)}, f32[]{:T(128)}, f32[]{:T(128)}, f32[]{:T(128)}, f32[4,64,512]{2,1,0:T(8,128)S(1)}) fusion(f32[4,64,512]{2,1,0:T(8,128)S(1)} %copy-done.4, f32[4,64,512]{2,1,0:T(8,128)S(1)} %copy-done, f32[4,64,512]{2,1,0:T(8,128)S(1)} %slice_multiply_fusion, f32[4,65,512]{2,1,0:T(8,128)S(1)} %fusion.11, ...), kind=kLoop, calls=%fused_computation.37 | loop fusion | flops 2490364 | bytes 4718608 | tf_op jit(solution)/shard_map/reduce_sum | solution.py:80
  27.7 5.6 %all-reduce.5 = (f32[]{:T(128)}, f32[]{:T(128)}, f32[]{:T(128)}, f32[]{:T(128)}) all-reduce(f32[]{:T(128)} %get-tuple-element.5, f32[]{:T(128)} %get-tuple-element.6, f32[]{:T(128)} %get-tuple-element.4, f32[]{:T(128)} %get-tuple-element.3), channel_id=1, replica_groups=mesh['il'=16,'xl'=2] {'xl'}, use_global_device_ids=true, to_apply=%region_1.2 | all-reduce | flops 4 | bytes 32 | tf_op jit(solution)/shard_map/psum | solution.py:10
  33.3 30.2 %all-reduce.4 = (f32[]{:T(128)}, f32[]{:T(128)}, f32[]{:T(128)}, f32[]{:T(128)}) all-reduce(f32[]{:T(128)} %get-tuple-element.11, f32[]{:T(128)} %get-tuple-element.12, f32[]{:T(128)} %get-tuple-element.13, f32[]{:T(128)} %get-tuple-element.14), channel_id=1, replica_groups=mesh['il'=16,'xl'=2] {'il'}, use_global_device_ids=true, to_apply=%region_2.3 | all-reduce | flops 4 | bytes 32 | tf_op jit(solution)/shard_map/psum | solution.py:11
  67.4 0.0 copy-done.5
  67.4 1.4 %multiply_add_fusion = (f32[4,64,512]{2,1,0:T(8,128)}, f32[4,64,512]{2,1,0:T(8,128)}, f32[4,64,512]{2,1,0:T(8,128)}) fusion(f32[4,64,512]{2,1,0:T(8,128)S(1)} %copy-done, f32[]{:T(128)S(6)} %div.7, f32[4,64,512]{2,1,0:T(8,128)S(1)} %copy-done.4, f32[4,64,512]{2,1,0:T(8,128)S(1)} %get-tuple-element.17, f32[]{:T(128)S(6)} %div.6, f32[4,64,512]{2,1,0:T(8,128)S(1)} %copy-done.5), kind=kLoop, calls=%fused_computation.36 | loop fusion | flops 786432 | bytes 3670024 | tf_op jit(solution)/shard_map/add | solution.py:89
  (11 shorter events, 0.1 us)
Async XLA Ops:
  0.6 4.8 %copy-start.1 = (f32[4,64,512]{2,1,0:T(8,128)S(1)}, f32[4,64,512]{2,1,0:T(8,128)}, u32[]{:S(2)}) copy-start(f32[4,64,512]{2,1,0:T(8,128)} %param.11) | copy-start | bytes 1572868
  1.7 14.1 %collective-permute-start.2 = (f32[1,64,512]{2,1,0:T(8,128)S(1)}, f32[1,64,512]{2,1,0:T(8,128)S(1)}, u32[]{:S(2)}, u32[]{:S(2)}) collective-permute-start(f32[1,64,512]{2,1,0:T(8,128)S(1)} %get-tuple-element.24), channel_id=1, source_target_pairs={{0,2},{2,4},{4,6},{6,8},{8,10},{10,12},{12,14},{14,16},{16,18},{18... | collective-permute-start | bytes 393224 | tf_op jit(solution)/shard_map/ppermute | solution.py:21
  4.1 11.8 %collective-permute-start.1 = (f32[1,64,512]{2,1,0:T(8,128)S(1)}, f32[1,64,512]{2,1,0:T(8,128)S(1)}, u32[]{:S(2)}, u32[]{:S(2)}) collective-permute-start(f32[1,64,512]{2,1,0:T(8,128)S(1)} %get-tuple-element.23), channel_id=1, source_target_pairs={{2,0},{4,2},{6,4},{8,6},{10,8},{12,10},{14,12},{16,14},{18,16},{20... | collective-permute-start | bytes 393224 | tf_op jit(solution)/shard_map/ppermute | solution.py:22
  6.3 11.2 %collective-permute-start.3 = (f32[2,4,1,512]{3,2,1,0:T(1,128)S(1)}, f32[2,4,1,512]{3,2,1,0:T(1,128)S(1)}, u32[]{:S(2)}, u32[]{:S(2)}) collective-permute-start(f32[2,4,1,512]{3,2,1,0:T(1,128)S(1)} %pad_maximum_fusion.3), channel_id=1, source_target_pairs={{0,1},{2,3},{4,5},{6,7},{8,9},{10,11},{12,13},{14,15},{16,17},{18,... | collective-permute-start | bytes 49160 | tf_op jit(solution)/shard_map/ppermute | solution.py:30
  11.5 4.3 %copy-start = (f32[4,64,512]{2,1,0:T(8,128)S(1)}, f32[4,64,512]{2,1,0:T(8,128)}, u32[]{:S(2)}) copy-start(f32[4,64,512]{2,1,0:T(8,128)} %param.8) | copy-start | bytes 1572868
  11.5 12.4 %collective-permute-start = (f32[2,1,64,512]{3,2,1,0:T(8,128)S(1)}, f32[2,1,64,512]{3,2,1,0:T(8,128)S(1)}, u32[]{:S(2)}, u32[]{:S(2)}) collective-permute-start(f32[2,1,64,512]{3,2,1,0:T(8,128)S(1)} %pad_maximum_fusion.2), channel_id=1, source_target_pairs={{0,2},{2,4},{4,6},{6,8},{8,10},{10,12},{12,14},{14,16},{16,18},{18... | collective-permute-start | bytes 786440 | tf_op jit(solution)/shard_map/ppermute | solution.py:30
  15.9 3.0 %collective-permute-start.5 = (f32[6,1,512]{2,1,0:T(1,128)S(1)}, f32[6,1,512]{2,1,0:T(1,128)S(1)}, u32[]{:S(2)}, u32[]{:S(2)}) collective-permute-start(f32[6,1,512]{2,1,0:T(1,128)S(1)} %get-tuple-element.19), channel_id=1, source_target_pairs={{0,1},{2,3},{4,5},{6,7},{8,9},{10,11},{12,13},{14,15},{16,17},{18,... | collective-permute-start | bytes 36872 | tf_op jit(solution)/shard_map/ppermute | solution.py:21
  17.5 5.7 %copy-start.3 = (f32[4,64,512]{2,1,0:T(8,128)S(1)}, f32[4,64,512]{2,1,0:T(8,128)}, u32[]{:S(2)}) copy-start(f32[4,64,512]{2,1,0:T(8,128)} %param.10) | copy-start | bytes 1572868
  17.5 5.7 %collective-permute-start.4 = (f32[6,1,512]{2,1,0:T(1,128)S(1)}, f32[6,1,512]{2,1,0:T(1,128)S(1)}, u32[]{:S(2)}, u32[]{:S(2)}) collective-permute-start(f32[6,1,512]{2,1,0:T(1,128)S(1)} %get-tuple-element.18), channel_id=1, source_target_pairs={{1,0},{3,2},{5,4},{7,6},{9,8},{11,10},{13,12},{15,14},{17,16},{19,... | collective-permute-start | bytes 36872 | tf_op jit(solution)/shard_map/ppermute | solution.py:22
  23.9 1.0 %copy-start.2 = (f32[4,64,512]{2,1,0:T(8,128)S(1)}, f32[4,64,512]{2,1,0:T(8,128)}, u32[]{:S(2)}) copy-start(f32[4,64,512]{2,1,0:T(8,128)} %param.9) | copy-start | bytes 1572868
  25.4 1.0 %copy-start.4 = (f32[4,64,512]{2,1,0:T(8,128)S(1)}, f32[4,64,512]{2,1,0:T(8,128)}, u32[]{:S(2)}) copy-start(f32[4,64,512]{2,1,0:T(8,128)} %param.7) | copy-start | bytes 1572868
  26.5 40.9 %copy-start.5 = (f32[4,64,512]{2,1,0:T(8,128)S(1)}, f32[4,64,512]{2,1,0:T(8,128)}, u32[]{:S(2)}) copy-start(f32[4,64,512]{2,1,0:T(8,128)} %param.6) | copy-start | bytes 1572868
